TPU v7x, 256 devices: a whole 4x4x8 slice. The times are simulated.
256 devices in a mesh: req: 32 (over x, y, core), tp: 8 (over z).
Axes of the slice: x: 4, y: 4, z: 8, core: 2. Of those that a mesh axis runs over, the one named last changes fastest.
Arguments:
- activations: bfloat16 [4096, 2560], P('req', 'tp'), may hold values from -12 to 12
- norm_gain: float32 [2560], replicated, may hold values from 0.1 to 1.9
- input_proj: bfloat16 [2560, 8, 480], P(None, 'tp'), may hold values from -0.125 to 0.125
- output_proj: bfloat16 [2560, 2560], P('tp'), may hold values from -0.125 to 0.125
- cache_pool: bfloat16 [3008, 8, 20480], P('req', 'tp'), may hold values from -103 to 103
- page_table: int32 [64, 32], replicated, may hold values from 0 to 93, as said below
- rebalance_plan: int32 [64, 32], replicated, may hold values from 0 to 31, as said below
- cached_lengths: int32 [64], replicated, may hold values from 1 to 4096, as said below
- token_positions: int32 [64, 64], replicated, may hold values from 1 to 4159, as said below
Outputs:
- attention_out: float32 [4096, 2560], P('req', 'tp')
Inputs may be any that keep to these rules, and one draw needn't show every extreme that they name: token_positions[r, t] = cached_lengths[r] + t. `cached_lengths`: cached tokens of request r before its new ones; in every draw all requests of some group have 4096. rebalance_plan[r, j] is the request's own group for j < 16 and another group for later pages; page 16 of the first request of group q lies in group (q + 16) % 32; at most 2 of the pages j >= 16 of one group's requests lie in any one other group, and some group receives 2 from one other group in every draw. `page_table`: slot of page j of request r in the pool of group rebalance_plan[r, j]; no two entries of the table name the same group and slot.
All inputs are finite; a program needn't handle non-finite values.
Results may differ from a plain program's by a relative error of at most 0.0095.
The roundings to bfloat16 on the way count: a program that leaves them out, or rounds other values in their place, can miss the bound.
Values may be sent and summed in bfloat16 or wider, within the bound.
A program may use at most 128 MiB of HBM per device.

v0:
```python
import jax
import jax.numpy as jnp
from jax import lax
from jax.sharding import PartitionSpec as P

HD = 80
WINDOW = 4096
PAGE = 128
KEEP = 16
NEW = 64
TAIL = 16
EPSILON = 1e-05
THETA = 10000.0
MASKED = -1e30


def rotate(values, places):
    half_dim = values.shape[-1] // 2
    frequency = THETA ** (-(jnp.arange(half_dim, dtype=jnp.float32) * 2.0 / values.shape[-1]))
    angles = places.astype(jnp.float32)[..., None] * frequency
    cosine = jnp.cos(angles)
    sine_part = jnp.sin(angles)
    front_half = values[..., :half_dim]
    back_half = values[..., half_dim:]
    return jnp.concatenate(
        [front_half * cosine - back_half * sine_part, back_half * cosine + front_half * sine_part],
        axis=-1,
    )


def page_valid(places, lengths_here, page_ids):
    key_pos = page_ids[:, :, None] * PAGE + jnp.arange(PAGE, dtype=jnp.int32)[None, None, :]
    inside = key_pos < lengths_here[:, None, None]
    in_window = places[:, None, :, None] - key_pos[:, :, None, :] < WINDOW
    return inside[:, :, None, :] & in_window


def page_stats(queries, pages, valid):
    head_dim = queries.shape[-1]
    unpacked = pages.reshape(pages.shape[:3] + (-1, 2, head_dim))
    cache_keys = unpacked[..., 0, :]
    cache_values = unpacked[..., 1, :]
    scores = jnp.einsum(
        "rtkgd,rjkpd->rjkgtp", queries, cache_keys, preferred_element_type=jnp.float32
    ) * head_dim ** (-0.5)
    valid_mask = valid[:, :, None, None]
    block_peaks = jnp.max(jnp.where(valid_mask, scores, MASKED), axis=-1)
    probabilities = jnp.where(valid_mask, jnp.exp(scores - block_peaks[..., None]), 0.0).astype(
        jnp.bfloat16
    )
    totals = jnp.sum(probabilities, axis=-1, dtype=jnp.float32)
    value_sums = jnp.einsum(
        "rjkgtp,rjkpd->rjkgtd", probabilities, cache_values, preferred_element_type=jnp.float32
    )
    return (block_peaks, totals, value_sums)


def new_stats(queries, new_keys, new_values):
    head_dim = queries.shape[-1]
    count = queries.shape[1]
    scores = jnp.einsum(
        "rtkgd,rukd->rkgtu", queries, new_keys, preferred_element_type=jnp.float32
    ) * head_dim ** (-0.5)
    causal = jnp.arange(count)[:, None] >= jnp.arange(count)[None, :]
    block_peaks = jnp.max(jnp.where(causal, scores, MASKED), axis=-1)
    probabilities = jnp.where(causal, jnp.exp(scores - block_peaks[..., None]), 0.0).astype(
        jnp.bfloat16
    )
    totals = jnp.sum(probabilities, axis=-1, dtype=jnp.float32)
    value_sums = jnp.einsum(
        "rkgtu,rukd->rkgtd", probabilities, new_values, preferred_element_type=jnp.float32
    )
    return (block_peaks, totals, value_sums)


def fold_blocks(block_peaks, totals, value_sums):
    top_peak = jnp.max(block_peaks, axis=1)
    weights = jnp.exp(block_peaks - top_peak[:, None])
    return (
        top_peak,
        jnp.sum(weights * totals, axis=1),
        jnp.sum(weights[..., None] * value_sums, axis=1),
    )


def join_pair(first_stats, second_stats):
    top_peak = jnp.maximum(first_stats[0], second_stats[0])
    weight_one = jnp.exp(first_stats[0] - top_peak)
    weight_two = jnp.exp(second_stats[0] - top_peak)
    totals = weight_one * first_stats[1] + weight_two * second_stats[1]
    value_sums = weight_one[..., None] * first_stats[2] + weight_two[..., None] * second_stats[2]
    return (top_peak, totals, value_sums)


def local(
    activations,
    norm_gain,
    input_proj,
    output_proj,
    cache_pool,
    page_table,
    rebalance_plan,
    cached_lengths,
    token_positions,
):
    group_index = lax.axis_index("req")
    group_count = lax.axis_size("req")
    tok_rows = activations.shape[0]
    req_here = tok_rows // NEW
    kv_local = input_proj.shape[1]
    model_width = input_proj.shape[0]
    group_size = input_proj.shape[2] // HD - 2
    gathered = lax.all_gather(activations, "tp", axis=1, tiled=True)
    widened = gathered.astype(jnp.float32)
    mean_square = jnp.mean(widened * widened, axis=1, keepdims=True)
    normed = (widened * lax.rsqrt(mean_square + EPSILON) * norm_gain).astype(jnp.bfloat16)
    projected = jnp.dot(
        normed, input_proj.reshape(model_width, -1), preferred_element_type=jnp.float32
    )
    projected = projected.reshape(tok_rows, kv_local, group_size + 2, HD)
    first_row = group_index * req_here
    my_places = lax.dynamic_slice_in_dim(token_positions, first_row, req_here, 0)
    my_lengths = lax.dynamic_slice_in_dim(cached_lengths, first_row, req_here, 0)
    my_table = lax.dynamic_slice_in_dim(page_table, first_row, req_here, 0)
    my_plan = lax.dynamic_slice_in_dim(rebalance_plan, first_row, req_here, 0)
    flat_places = my_places.reshape(tok_rows)
    queries = rotate(
        projected[:, :, :group_size],
        jnp.broadcast_to(flat_places[:, None, None], (tok_rows, kv_local, group_size)),
    )
    queries = queries.astype(jnp.bfloat16).reshape(req_here, NEW, kv_local, group_size, HD)
    new_keys = rotate(projected[:, :, group_size], flat_places[:, None])
    new_keys = new_keys.astype(jnp.bfloat16).reshape(req_here, NEW, kv_local, HD)
    new_values = (
        projected[:, :, group_size + 1].astype(jnp.bfloat16).reshape(req_here, NEW, kv_local, HD)
    )
    fresh_stats = new_stats(queries, new_keys, new_values)
    tail_len = TAIL
    entries = req_here * tail_len
    capacity = (entries + group_count - 2) // (group_count - 1)
    home_ids = jnp.broadcast_to(jnp.arange(KEEP, dtype=jnp.int32)[None, :], (req_here, KEEP))
    tail_ids = jnp.broadcast_to(
        KEEP + jnp.arange(tail_len, dtype=jnp.int32)[None, :], (req_here, tail_len)
    )
    home_pages = cache_pool[my_table[:, :KEEP]]
    tail_plan = rebalance_plan[:, KEEP:].reshape(group_count, entries)
    tail_table = page_table[:, KEEP:].reshape(group_count, entries)
    held_here = tail_plan == group_index
    held_rank = jnp.cumsum(held_here.astype(jnp.int32), axis=1) - 1
    picked = held_here[:, :, None] & (
        held_rank[:, :, None] == jnp.arange(capacity, dtype=jnp.int32)[None, None, :]
    )
    entry_ids = jnp.sum(
        jnp.where(picked, jnp.arange(entries, dtype=jnp.int32)[None, :, None], 0), axis=1
    )
    send_slots = jnp.take_along_axis(tail_table, entry_ids, axis=1)
    outgoing = cache_pool[send_slots]
    own_plan = my_plan[:, KEEP:].reshape(entries)
    at_group = own_plan[:, None] == jnp.arange(group_count, dtype=jnp.int32)[None, :]
    own_rank = jnp.sum(
        jnp.where(at_group, jnp.cumsum(at_group.astype(jnp.int32), axis=0) - 1, 0), axis=1
    )
    flat_index = own_plan * capacity + own_rank
    received = lax.all_to_all(outgoing, "req", split_axis=0, concat_axis=0, tiled=True)
    tail_pages = received.reshape(group_count * capacity, kv_local, -1)[flat_index].reshape(
        req_here, tail_len, kv_local, -1
    )
    dense_pages = jnp.concatenate([home_pages, tail_pages], axis=1)
    all_ids = jnp.concatenate([home_ids, tail_ids], axis=1)
    combined = fold_blocks(
        *page_stats(queries, dense_pages, page_valid(my_places, my_lengths, all_ids))
    )
    merged = join_pair(combined, fresh_stats)
    heads_out = merged[2] / merged[1][..., None]
    heads_out = jnp.transpose(heads_out, (0, 3, 1, 2, 4)).reshape(tok_rows, -1).astype(jnp.bfloat16)
    partial_value = jnp.dot(heads_out, output_proj, preferred_element_type=jnp.float32)
    return lax.psum_scatter(partial_value, "tp", scatter_dimension=1, tiled=True)


def solution(mesh):
    in_specs = (
        P("req", "tp"),
        P(),
        P(None, "tp", None),
        P("tp", None),
        P("req", "tp", None),
        P(),
        P(),
        P(),
        P(),
    )
    out_specs = P("req", "tp")
    return jax.shard_map(local, mesh=mesh, in_specs=in_specs, out_specs=out_specs, check_vma=False)
```

profile of v0, /device:TPU:4, one launch (start us, length us, event | category | flops | bytes accessed | tf_op | source)
XLA Modules:
  0.0 170.4 jit_solution(8499491559643690964)
XLA Ops:
  6.5 0.9 slice_compare_fusion
  7.6 0.7 slice.42
  8.3 0.2 reduce_window_sum.22
  9.0 0.8 gather_fusion.3
  10.2 8.6 %gather_fusion.1 = bf16[64,20480]{1,0:T(8,128)(2,1)} fusion(bf16[94,20480]{1,0:T(8,128)(2,1)} %bitcast.127, s32[1024]{0:T(1024)S(1)} %pad_clamp_fusion.1), kind=kCustom, calls=%fused_computation.1 | custom fusion | bytes 5243136 | tf_op jit(solution)/shard_map/gather | solution.py:157
  18.8 4.8 %reshape.491 = bf16[32,2,1,20480]{3,1,0,2:T(2,128)(2,1)} reshape(bf16[64,20480]{1,0:T(8,128)(2,1)} %gather_fusion.1) | data formatting | bytes 5242880 | tf_op jit(solution)/shard_map/gather | solution.py:157
  23.6 7.8 %all-to-all-start = ((bf16[32,2,1,20480]{3,1,2,0:T(2,128)(2,1)}), bf16[32,2,1,20480]{3,1,2,0:T(2,128)(2,1)}, u32[]{:S(2)}, u32[]{:S(2)}) async-start(bf16[32,2,1,20480]{3,1,2,0:T(2,128)(2,1)} %bitcast.129), calls=%async_computation | async-start | bytes 5242880 | tf_op jit(solution)/shard_map/all_to_all | solution.py:164
  31.8 1.2 fusion.61
  33.1 29.3 %all_gather.3 = bf16[128,2560]{0,1:T(8,128)(2,1)S(1)} all-gather(bf16[128,320]{0,1:T(8,128)(2,1)S(1)} %copy-done.3), channel_id=1, replica_groups=mesh['req'=32,'tp'=8] {'tp'}, dimensions={1}, use_global_device_ids=true | all-gather | bytes 737280 | tf_op jit(solution)/shard_map/all_gather | solution.py:113
  62.3 0.4 fusion.10
  62.7 0.9 convolution_bitcast_fusion
  64.3 0.2 fusion.47
  64.8 0.2 fusion.36
  65.1 0.1 copy.90
  65.3 0.1 copy.91
  65.4 6.2 %gather_fusion = bf16[32,20480]{1,0:T(8,128)(2,1)} fusion(bf16[94,20480]{1,0:T(8,128)(2,1)} %bitcast.128, s32[1024]{0:T(1024)S(1)} %pad_clamp_fusion.2), kind=kCustom, calls=%fused_computation | custom fusion | bytes 2621568 | tf_op jit(solution)/shard_map/gather | solution.py:145
  71.7 4.5 %concatenate.44 = bf16[2,16,1,128,2,80]{5,4,3,1,0,2:T(2,128)(2,1)} reshape(bf16[32,20480]{1,0:T(8,128)(2,1)} %gather_fusion) | data formatting | bytes 2621440 | tf_op jit(solution)/shard_map/concatenate | solution.py:168
  76.2 5.9 %copy.87 = bf16[2,16,1,128,2,80]{3,5,1,0,4,2:T(8,128)(2,1)} copy(bf16[2,16,1,128,2,80]{5,4,3,1,0,2:T(2,128)(2,1)} %concatenate.44) | data formatting | bytes 2621440 | tf_op jit(solution)/shard_map/concatenate | solution.py:168
  82.1 0.2 select_reduce_fusion.2
  82.3 0.6 pad_clamp_fusion
  82.9 0.3 select_reduce_fusion
  83.5 1.2 fusion.9
  84.7 4.4 %reshape.500 = bf16[64,20480]{1,0:T(8,128)(2,1)} reshape(bf16[32,2,1,20480]{3,1,2,0:T(2,128)(2,1)} %all-to-all-done) | data formatting | bytes 5242880 | tf_op jit(solution)/shard_map/reshape | solution.py:165
  89.1 5.8 %gather_fusion.2 = bf16[32,20480]{1,0:T(8,128)(2,1)} fusion(bf16[64,20480]{1,0:T(8,128)(2,1)} %reshape.500, s32[1024]{0:T(1024)} %pad_clamp_fusion), kind=kCustom, calls=%fused_computation.2 | custom fusion | bytes 2621568 | tf_op jit(solution)/shard_map/gather | solution.py:165
  94.9 4.5 %concatenate.45 = bf16[2,16,1,128,2,80]{5,4,3,1,0,2:T(2,128)(2,1)} reshape(bf16[32,20480]{1,0:T(8,128)(2,1)} %gather_fusion.2) | data formatting | bytes 2621440 | tf_op jit(solution)/shard_map/concatenate | solution.py:168
  99.5 5.9 %copy.88 = bf16[2,16,1,128,2,80]{3,5,1,0,4,2:T(8,128)(2,1)} copy(bf16[2,16,1,128,2,80]{5,4,3,1,0,2:T(2,128)(2,1)} %concatenate.45) | data formatting | bytes 2621440 | tf_op jit(solution)/shard_map/concatenate | solution.py:168
  105.4 4.0 %fusion.3 = (f32[2,32,4,64]{3,2,1,0:T(4,128)S(1)}, f32[2,32,128,64,4]{2,3,4,1,0:T(8,128)S(1)}) fusion(pred[2,32,64,128]{3,2,1,0:T(8,128)(4,1)S(1)} %fusion.9, bf16[2,64,4,40]{3,1,2,0:T(8,128)(2,1)S(1)} %copy.91, bf16[2,64,4,40]{3,1,2,0:T(8,128)(2,1)S(1)} %copy.90, bf16[2,16,1,128,2,80]{3,5,1,0,4,2:T(8,128)(2,1)} %copy.87, ...), kind=kOutput, calls=%fused_computation.11 | convolution fusion | flops 344604672 | bytes 11681792 | tf_op jit(solution)/shard_map/rtkgd,rjkpd->rjkgtp/dot_general | solution.py:43
  109.4 5.8 %convert_reduce_fusion = (f32[2,32,4,64]{3,2,1,0:T(4,128)S(1)}, f32[2,4,64]{2,1,0:T(4,128)S(1)}) fusion(f32[2,32,4,64]{3,2,1,0:T(4,128)S(1)} %get-tuple-element.18, f32[2,32,128,64,4]{2,3,4,1,0:T(8,128)S(1)} %get-tuple-element.19, pred[2,32,64,128]{3,2,1,0:T(8,128)(4,1)S(1)} %fusion.9), kind=kLoop, calls=%fused_computation.9 | loop fusion | flops 16760320 | bytes 9046016 | tf_op jit(solution)/shard_map/reduce_sum | solution.py:51
  115.4 5.1 %multiply_reduce_fusion = f32[2,4,64,80]{3,2,1,0:T(8,128)S(1)} fusion(f32[2,32,4,64]{3,2,1,0:T(4,128)S(1)} %get-tuple-element.11, bf16[2,16,1,128,2,80]{3,5,1,0,4,2:T(8,128)(2,1)S(1)} %copy-done.2, bf16[2,16,1,128,2,80]{3,5,1,0,4,2:T(8,128)(2,1)S(1)} %copy-done.1, f32[2,32,128,64,4]{2,3,4,1,0:T(8,128)S(1)} %get-tuple-element.19, ...), kind=kOutput, calls=%fused_computation.10 | convolution fusion | flops 347168768 | bytes 11829248 | tf_op jit(solution)/shard_map/rjkgtp,rjkpd->rjkgtd/dot_general | solution.py:52
  120.5 0.3 fusion.24
  121.1 3.4 %fusion.62 = f32[128,2560]{0,1:T(8,128)} fusion(bf16[128,320]{1,0:T(8,128)(2,1)S(1)} %convert_element_type.92, bf16[320,2560]{1,0:T(8,128)(2,1)} %param.12), kind=kOutput, calls=%fused_computation.112 | convolution fusion | flops 209715200 | bytes 3031040 | tf_op jit(solution)/shard_map/dot_general | solution.py:176
  124.5 39.0 %reduce-scatter.2.cloned.1.call-done = f32[128,320]{0,1:T(8,128)} async-done(((f32[128,2560]{0,1:T(8,128)}), f32[128,320]{0,1:T(8,128)}) %reduce-scatter.2.cloned.1.call-update) | async-done | bytes 163856 | tf_op jit(solution)/shard_map/reduce_scatter | solution.py:177
  (70 shorter events, 3.3 us)
Async XLA Ops:
  6.5 56.2 %copy-start = (bf16[2560,1,480]{0,2,1:T(8,128)(2,1)S(1)}, bf16[2560,1,480]{0,2,1:T(8,128)(2,1)}, u32[]{:S(2)}) copy-start(bf16[2560,1,480]{0,2,1:T(8,128)(2,1)} %param.11) | copy-start | bytes 7372804
  23.6 7.9 %copy-start.4 = (s32[64,32]{0,1:T(8,128)S(1)}, s32[64,32]{0,1:T(8,128)}, u32[]{:S(2)}) copy-start(s32[64,32]{0,1:T(8,128)} %param.15) | copy-start | bytes 24580
  23.6 8.2 %copy-start.5 = (s32[64,32]{0,1:T(8,128)S(1)}, s32[64,32]{0,1:T(8,128)}, u32[]{:S(2)}) copy-start(s32[64,32]{0,1:T(8,128)} %param.14) | copy-start | bytes 24580
  23.6 9.5 %copy-start.3 = (bf16[128,320]{0,1:T(8,128)(2,1)S(1)}, bf16[128,320]{0,1:T(8,128)(2,1)}, u32[]{:S(2)}) copy-start(bf16[128,320]{0,1:T(8,128)(2,1)} %param.9) | copy-start | bytes 245764
  23.6 39.2 %copy-start.6 = (f32[2560]{0:T(1024)S(1)}, f32[2560]{0:T(1024)}, u32[]{:S(2)}) copy-start(f32[2560]{0:T(1024)} %param.10) | copy-start | bytes 30724
  23.6 61.1 %all-to-all-start = ((bf16[32,2,1,20480]{3,1,2,0:T(2,128)(2,1)}), bf16[32,2,1,20480]{3,1,2,0:T(2,128)(2,1)}, u32[]{:S(2)}, u32[]{:S(2)}) async-start(bf16[32,2,1,20480]{3,1,2,0:T(2,128)(2,1)} %bitcast.129), calls=%async_computation | async-start | bytes 5242880 | tf_op jit(solution)/shard_map/all_to_all | solution.py:164
  31.4 32.3 %copy-start.7 = (s32[64]{0:T(128)S(1)}, s32[64]{0:T(128)}, u32[]{:S(2)}) copy-start(s32[64]{0:T(128)} %param.16) | copy-start | bytes 772
  31.4 132.2 %reduce-scatter.2.cloned.1.call-start = ((), (), s32[]{:S(2)}) async-start(), calls=%async_computation.2 | async-start | bytes 1474560 | tf_op jit(solution)/shard_map/reduce_scatter | solution.py:177
  109.4 5.9 %copy-start.1 = (bf16[2,16,1,128,2,80]{3,5,1,0,4,2:T(8,128)(2,1)S(1)}, bf16[2,16,1,128,2,80]{3,5,1,0,4,2:T(8,128)(2,1)}, u32[]{:S(2)}) copy-start(bf16[2,16,1,128,2,80]{3,5,1,0,4,2:T(8,128)(2,1)} %copy.87) | copy-start | bytes 3932164
  109.4 5.9 %copy-start.2 = (bf16[2,16,1,128,2,80]{3,5,1,0,4,2:T(8,128)(2,1)S(1)}, bf16[2,16,1,128,2,80]{3,5,1,0,4,2:T(8,128)(2,1)}, u32[]{:S(2)}) copy-start(bf16[2,16,1,128,2,80]{3,5,1,0,4,2:T(8,128)(2,1)} %copy.88) | copy-start | bytes 3932164
Sparse Core Ops, SparseCore 0:
  124.6 38.8 reduce-scatter.1
where the time goes:
time: 171 us; the launch traced here: 170 us
  local copies, waits for them, and re-layouts  55 us (32%)
  waiting for transfers between devices  39 us (23%)
  blocking collectives  29.3 us (17%)
  matrix products  14.1 us (8%)
  between operations  13.7 us (8%)
  other arithmetic  11.5 us (7%)
  starting transfers between devices  7.83 us (5%)
    reduce_scatter x1, waiting for transfers between devices, local(): lax.psum_scatter(partial_value, 'tp', scatter_dimension=1, tiled=True)  39 us
    all_gather x1, blocking collectives, local(): gathered = lax.all_gather(activations, 'tp', axis=1, tiled=True)  29.3 us
    concatenate x4, local copies, waits for them, and re-layouts, local(): dense_pages = jnp.concatenate([home_pages, tail_pages], axis=1)  20.9 us
    gather x2, local copies, waits for them, and re-layouts, local(): outgoing = cache_pool[send_slots]  13.3 us
    all_to_all x1, starting transfers between devices, local(): lax.all_to_all(outgoing, 'req', split_axis=0, concat_axis=0, tiled=True)  7.79 us
    gather x1, local copies, waits for them, and re-layouts, local(): home_pages = cache_pool[my_table[:, :KEEP]]  6.23 us
    reduce_sum x1, other arithmetic, page_stats(): totals = jnp.sum(probabilities, axis=-1, dtype=jnp.float32)  5.84 us
    gather x1, local copies, waits for them, and re-layouts, local(): received.reshape(group_count * capacity, kv_local, -1)[flat_index]  5.8 us
  transfers between devices with their start and end apart: 2, of which 1 were waited for; matrix products, arithmetic and copies ran while one was open for 14% of the time, Pallas kernels for 0%

commit v1 on v0

--- a/solution.py
+++ b/solution.py
@@ -2,6 +2,7 @@
 import jax.numpy as jnp
 from jax import lax
 from jax.sharding import PartitionSpec as P
+from jax.lax import axis_index, axis_size, ppermute
 
 HD = 80
 WINDOW = 4096
@@ -110,7 +111,26 @@
     kv_local = input_proj.shape[1]
     model_width = input_proj.shape[0]
     group_size = input_proj.shape[2] // HD - 2
-    gathered = lax.all_gather(activations, "tp", axis=1, tiled=True)
+    outcome_arr, formed, x_new = (axis_size("tp"), axis_index("tp"), activations.shape[1])
+    row_list = [(it, (it + 1) % outcome_arr) for it in range(outcome_arr)]
+    gathered = jnp.zeros(
+        (*activations.shape[:1], outcome_arr * x_new, *activations.shape[1 + 1 :]),
+        activations.dtype,
+    )
+    history = [(it, (it - 1) % outcome_arr) for it in range(outcome_arr)]
+    gathered = lax.dynamic_update_slice_in_dim(gathered, activations, formed * x_new, axis=1)
+    mat_out = moved = activations
+    w_next = outcome_arr // 2
+    for dd in range(1, w_next + 1):
+        mat_out = ppermute(mat_out, perm=row_list, axis_name="tp")
+        gathered = lax.dynamic_update_slice_in_dim(
+            gathered, mat_out, (formed - dd) % outcome_arr * x_new, axis=1
+        )
+        if dd < outcome_arr - w_next:
+            moved = ppermute(moved, axis_name="tp", perm=history)
+            gathered = lax.dynamic_update_slice_in_dim(
+                gathered, moved, (formed + dd) % outcome_arr * x_new, axis=1
+            )
     widened = gathered.astype(jnp.float32)
     mean_square = jnp.mean(widened * widened, axis=1, keepdims=True)
     normed = (widened * lax.rsqrt(mean_square + EPSILON) * norm_gain).astype(jnp.bfloat16)

time: 171 us -> 171 us (level)
  blocking collectives: 29.3 us -> 0 us
  starting transfers between devices: 7.83 us -> 20.5 us
  local copies, waits for them, and re-layouts: 55 us -> 66.4 us
  waiting for transfers between devices: 39 us -> 42.9 us
    all_gather x1 -> x0, blocking collectives: 29.3 us -> none  [local(): gathered = lax.all_gather(activations, 'tp', axis=1, tiled=True)]
    ppermute x0 -> x7, starting transfers between devices: none -> 12.5 us  [the longest x3 12.4 us: local(): moved = ppermute(moved, axis_name='tp', perm=history)]
    dynamic_update_slice x0 -> x8, local copies, waits for them, and re-layouts: none -> 7.21 us  [the longest x4 3.46 us: local(): lax.dynamic_update_slice_in_dim(gathered, mat_out, (formed - dd) % outcom...]
    ppermute x0 -> x7, waiting for transfers between devices: none -> 4.45 us  [the longest x4 4.44 us: local(): mat_out = ppermute(mat_out, perm=row_list, axis_name='tp')]
    ppermute x0 -> x7, local copies, waits for them, and re-layouts: none -> 3.49 us  [the longest x4 2.25 us: local(): mat_out = ppermute(mat_out, perm=row_list, axis_name='tp')]
  transfers between devices with their start and end apart: 2 -> 9, of which waited for: 1 -> 3; matrix products, arithmetic and copies ran while one was open for 14% -> 31% of each run, Pallas kernels for 0% -> 0%
where the time goes in v1:
time: 171 us; the launch traced here: 170 us
  local copies, waits for them, and re-layouts  66.4 us (39%)
  waiting for transfers between devices  42.9 us (25%)
  starting transfers between devices  20.5 us (12%)
  matrix products  14 us (8%)
  between operations  13.9 us (8%)
  other arithmetic  11.9 us (7%)
    reduce_scatter x1, waiting for transfers between devices, local(): lax.psum_scatter(partial_value, 'tp', scatter_dimension=1, tiled=True)  38.4 us
    concatenate x4, local copies, waits for them, and re-layouts, local(): dense_pages = jnp.concatenate([home_pages, tail_pages], axis=1)  21 us
    gather x2, local copies, waits for them, and re-layouts, local(): outgoing = cache_pool[send_slots]  13.3 us
    ppermute x3, starting transfers between devices, local(): moved = ppermute(moved, axis_name='tp', perm=history)  12.4 us
    all_to_all x1, starting transfers between devices, local(): lax.all_to_all(outgoing, 'req', split_axis=0, concat_axis=0, tiled=True)  7.79 us
    gather x1, local copies, waits for them, and re-layouts, local(): home_pages = cache_pool[my_table[:, :KEEP]]  6.22 us
    reduce_sum x1, other arithmetic, page_stats(): totals = jnp.sum(probabilities, axis=-1, dtype=jnp.float32)  5.84 us
    gather x1, local copies, waits for them, and re-layouts, local(): received.reshape(group_count * capacity, kv_local, -1)[flat_index]  5.68 us
  transfers between devices with their start and end apart: 9, of which 3 were waited for; matrix products, arithmetic and copies ran while one was open for 31% of the time, Pallas kernels for 0%

profile of v1, /device:TPU:4, one launch (start us, length us, event | category | flops | bytes accessed | tf_op | source)
XLA Modules:
  0.0 169.6 jit_solution(5167745974441755544)
XLA Ops:
  6.5 5.9 %collective-permute-start.1 = (bf16[128,320]{0,1:T(8,128)(2,1)}, bf16[128,320]{0,1:T(8,128)(2,1)S(1)}, u32[]{:S(2)}, u32[]{:S(2)}) collective-permute-start(bf16[128,320]{0,1:T(8,128)(2,1)} %param.9), channel_id=1, source_target_pairs={{0,7},{1,0},{2,1},{3,2},{4,3},{5,4},{6,5},{7,6},{8,15},{9,8},{10,9... | collective-permute-start | bytes 245768 | tf_op jit(solution)/shard_map/ppermute | solution.py:130
  14.7 0.8 gather_fusion.3
  15.9 8.6 %gather_fusion.1 = bf16[64,20480]{1,0:T(8,128)(2,1)} fusion(bf16[94,20480]{1,0:T(8,128)(2,1)} %bitcast.127, s32[1024]{0:T(1024)S(1)} %pad_clamp_fusion.1), kind=kCustom, calls=%fused_computation.1 | custom fusion | bytes 5243136 | tf_op jit(solution)/shard_map/gather | solution.py:177
  24.5 4.8 %reshape.491 = bf16[32,2,1,20480]{3,1,0,2:T(2,128)(2,1)} reshape(bf16[64,20480]{1,0:T(8,128)(2,1)} %gather_fusion.1) | data formatting | bytes 5242880 | tf_op jit(solution)/shard_map/gather | solution.py:177
  29.3 7.8 %all-to-all-start = ((bf16[32,2,1,20480]{3,1,2,0:T(2,128)(2,1)}), bf16[32,2,1,20480]{3,1,2,0:T(2,128)(2,1)}, u32[]{:S(2)}, u32[]{:S(2)}) async-start(bf16[32,2,1,20480]{3,1,2,0:T(2,128)(2,1)} %bitcast.129), calls=%async_computation | async-start | bytes 5242880 | tf_op jit(solution)/shard_map/all_to_all | solution.py:184
  40.0 1.4 fusion.9
  41.4 6.2 %gather_fusion = bf16[32,20480]{1,0:T(8,128)(2,1)} fusion(bf16[94,20480]{1,0:T(8,128)(2,1)} %bitcast.128, s32[1024]{0:T(1024)S(1)} %pad_clamp_fusion.2), kind=kCustom, calls=%fused_computation | custom fusion | bytes 2621568 | tf_op jit(solution)/shard_map/gather | solution.py:165
  47.6 4.5 %concatenate.44 = bf16[2,16,1,128,2,80]{5,4,3,1,0,2:T(2,128)(2,1)} reshape(bf16[32,20480]{1,0:T(8,128)(2,1)} %gather_fusion) | data formatting | bytes 2621440 | tf_op jit(solution)/shard_map/concatenate | solution.py:188
  52.1 5.9 %copy.115 = bf16[2,16,1,128,2,80]{3,5,1,0,4,2:T(8,128)(2,1)} copy(bf16[2,16,1,128,2,80]{5,4,3,1,0,2:T(2,128)(2,1)} %concatenate.44) | data formatting | bytes 2621440 | tf_op jit(solution)/shard_map/concatenate | solution.py:188
  58.1 0.8 dynamic_update_slice.24
  59.0 3.3 %collective-permute-start.3 = (bf16[128,320]{0,1:T(8,128)(2,1)S(1)}, bf16[128,320]{0,1:T(8,128)(2,1)S(1)}, u32[]{:S(2)}, u32[]{:S(2)}) collective-permute-start(bf16[128,320]{0,1:T(8,128)(2,1)S(1)} %collective-permute-done.1), channel_id=1, source_target_pairs={{0,7},{1,0},{2,1},{3,2},{4,3},{5,4},{6,5},{7,6},{8,15},{9,8},{10,9... | collective-permute-start | bytes 245768 | tf_op jit(solution)/shard_map/ppermute | solution.py:130
  62.4 2.6 %collective-permute-done.2 = bf16[128,320]{0,1:T(8,128)(2,1)S(1)} collective-permute-done((bf16[128,320]{0,1:T(8,128)(2,1)S(1)}, bf16[128,320]{0,1:T(8,128)(2,1)S(1)}, u32[]{:S(2)}, u32[]{:S(2)}) %collective-permute-start.2) | collective-permute-done | bytes 81952 | tf_op jit(solution)/shard_map/ppermute | solution.py:125
  65.6 3.2 %collective-permute-start.5 = (bf16[128,320]{0,1:T(8,128)(2,1)S(1)}, bf16[128,320]{0,1:T(8,128)(2,1)}, u32[]{:S(2)}, u32[]{:S(2)}) collective-permute-start(bf16[128,320]{0,1:T(8,128)(2,1)S(1)} %collective-permute-done.3), channel_id=1, source_target_pairs={{0,7},{1,0},{2,1},{3,2},{4,3},{5,4},{6,5},{7,6},{8,15},{9,8},{10,9... | collective-permute-start | bytes 245768 | tf_op jit(solution)/shard_map/ppermute | solution.py:130
  68.8 1.8 %collective-permute-done.4 = bf16[128,320]{0,1:T(8,128)(2,1)S(1)} collective-permute-done((bf16[128,320]{0,1:T(8,128)(2,1)S(1)}, bf16[128,320]{0,1:T(8,128)(2,1)S(1)}, u32[]{:S(2)}, u32[]{:S(2)}) %collective-permute-start.4) | collective-permute-done | bytes 81952 | tf_op jit(solution)/shard_map/ppermute | solution.py:125
  71.3 0.8 dynamic_update_slice.25
  72.3 1.1 dynamic_update_slice.26
  73.4 1.0 copy.120
  76.2 1.1 dynamic_update_slice.29
  77.3 1.0 copy.123
  78.3 1.1 dynamic_update_slice.30
  79.4 1.0 copy.124
  80.4 0.8 dynamic_update_slice.31
  81.5 0.9 convolution_bitcast_fusion
  84.6 4.4 %reshape.500 = bf16[64,20480]{1,0:T(8,128)(2,1)} reshape(bf16[32,2,1,20480]{3,1,2,0:T(2,128)(2,1)} %all-to-all-done) | data formatting | bytes 5242880 | tf_op jit(solution)/shard_map/reshape | solution.py:185
  89.0 5.7 %gather_fusion.2 = bf16[32,20480]{1,0:T(8,128)(2,1)} fusion(bf16[64,20480]{1,0:T(8,128)(2,1)} %reshape.500, s32[1024]{0:T(1024)S(1)} %pad_clamp_fusion), kind=kCustom, calls=%fused_computation.2 | custom fusion | bytes 2621568 | tf_op jit(solution)/shard_map/gather | solution.py:185
  94.7 4.5 %concatenate.45 = bf16[2,16,1,128,2,80]{5,4,3,1,0,2:T(2,128)(2,1)} reshape(bf16[32,20480]{1,0:T(8,128)(2,1)} %gather_fusion.2) | data formatting | bytes 2621440 | tf_op jit(solution)/shard_map/concatenate | solution.py:188
  99.2 6.0 %copy.116 = bf16[2,16,1,128,2,80]{3,5,1,0,4,2:T(8,128)(2,1)} copy(bf16[2,16,1,128,2,80]{5,4,3,1,0,2:T(2,128)(2,1)} %concatenate.45) | data formatting | bytes 2621440 | tf_op jit(solution)/shard_map/concatenate | solution.py:188
  105.2 4.0 %fusion.3 = (f32[2,32,4,64]{3,2,1,0:T(4,128)S(1)}, f32[2,32,128,64,4]{2,3,4,1,0:T(8,128)S(1)}) fusion(pred[2,32,64,128]{3,2,1,0:T(8,128)(4,1)S(1)} %copy-done.1, bf16[2,64,4,40]{3,1,2,0:T(8,128)(2,1)S(1)} %copy.126, bf16[2,64,4,40]{3,1,2,0:T(8,128)(2,1)S(1)} %copy.125, bf16[2,16,1,128,2,80]{3,5,1,0,4,2:T(8,128)(2,1)} %copy.115, ...), kind=kOutput, calls=%fused_computation.11 | convolution fusion | flops 344604672 | bytes 11681792 | tf_op jit(solution)/shard_map/rtkgd,rjkpd->rjkgtp/dot_general | solution.py:44
  109.2 5.8 %convert_reduce_fusion = (f32[2,32,4,64]{3,2,1,0:T(4,128)S(1)}, f32[2,4,64]{2,1,0:T(4,128)S(1)}) fusion(f32[2,32,4,64]{3,2,1,0:T(4,128)S(1)} %get-tuple-element.18, f32[2,32,128,64,4]{2,3,4,1,0:T(8,128)S(1)} %get-tuple-element.19, pred[2,32,64,128]{3,2,1,0:T(8,128)(4,1)S(1)} %copy-done.1), kind=kLoop, calls=%fused_computation.9 | loop fusion | flops 16760320 | bytes 9046016 | tf_op jit(solution)/shard_map/reduce_sum | solution.py:52
  115.2 5.1 %multiply_reduce_fusion = f32[2,4,64,80]{3,2,1,0:T(8,128)S(1)} fusion(f32[2,32,4,64]{3,2,1,0:T(4,128)S(1)} %get-tuple-element.11, bf16[2,16,1,128,2,80]{3,5,1,0,4,2:T(8,128)(2,1)S(1)} %copy-done.3, bf16[2,16,1,128,2,80]{3,5,1,0,4,2:T(8,128)(2,1)S(1)} %copy-done.2, f32[2,32,128,64,4]{2,3,4,1,0:T(8,128)S(1)} %get-tuple-element.19, ...), kind=kOutput, calls=%fused_computation.10 | convolution fusion | flops 347168768 | bytes 11829248 | tf_op jit(solution)/shard_map/rjkgtp,rjkpd->rjkgtd/dot_general | solution.py:53
  120.9 3.4 %fusion.62 = f32[128,2560]{0,1:T(8,128)} fusion(bf16[128,320]{1,0:T(8,128)(2,1)S(1)} %convert_element_type.92, bf16[320,2560]{1,0:T(8,128)(2,1)} %param.12), kind=kOutput, calls=%fused_computation.112 | convolution fusion | flops 209715200 | bytes 3031040 | tf_op jit(solution)/shard_map/dot_general | solution.py:196
  124.4 38.4 %reduce-scatter.2.cloned.1.call-done = f32[128,320]{0,1:T(8,128)} async-done(((f32[128,2560]{0,1:T(8,128)}), f32[128,320]{0,1:T(8,128)}) %reduce-scatter.2.cloned.1.call-update) | async-done | bytes 163856 | tf_op jit(solution)/shard_map/reduce_scatter | solution.py:197
  (108 shorter events, 12.0 us)
Async XLA Ops:
  6.5 74.9 %copy-start = (bf16[2560,1,480]{0,2,1:T(8,128)(2,1)S(1)}, bf16[2560,1,480]{0,2,1:T(8,128)(2,1)}, u32[]{:S(2)}) copy-start(bf16[2560,1,480]{0,2,1:T(8,128)(2,1)} %param.11) | copy-start | bytes 7372804
  6.5 52.5 %collective-permute-start.1 = (bf16[128,320]{0,1:T(8,128)(2,1)}, bf16[128,320]{0,1:T(8,128)(2,1)S(1)}, u32[]{:S(2)}, u32[]{:S(2)}) collective-permute-start(bf16[128,320]{0,1:T(8,128)(2,1)} %param.9), channel_id=1, source_target_pairs={{0,7},{1,0},{2,1},{3,2},{4,3},{5,4},{6,5},{7,6},{8,15},{9,8},{10,9... | collective-permute-start | bytes 245768 | tf_op jit(solution)/shard_map/ppermute | solution.py:130
  12.4 46.5 %collective-permute-start = (bf16[128,320]{0,1:T(8,128)(2,1)}, bf16[128,320]{0,1:T(8,128)(2,1)S(1)}, u32[]{:S(2)}, u32[]{:S(2)}) collective-permute-start(bf16[128,320]{0,1:T(8,128)(2,1)} %param.9), channel_id=1, source_target_pairs={{0,1},{1,2},{2,3},{3,4},{4,5},{5,6},{6,7},{7,0},{8,9},{9,10},{10,1... | collective-permute-start | bytes 245768 | tf_op jit(solution)/shard_map/ppermute | solution.py:125
  29.3 8.1 %copy-start.7 = (s32[64,32]{0,1:T(8,128)S(1)}, s32[64,32]{0,1:T(8,128)}, u32[]{:S(2)}) copy-start(s32[64,32]{0,1:T(8,128)} %param.15) | copy-start | bytes 24580
  29.3 8.3 %copy-start.8 = (s32[64,32]{0,1:T(8,128)S(1)}, s32[64,32]{0,1:T(8,128)}, u32[]{:S(2)}) copy-start(s32[64,32]{0,1:T(8,128)} %param.14) | copy-start | bytes 24580
  29.3 8.4 %copy-start.11 = (s32[64]{0:T(128)S(1)}, s32[64]{0:T(128)}, u32[]{:S(2)}) copy-start(s32[64]{0:T(128)} %param.16) | copy-start | bytes 772
  29.3 10.3 %copy-start.4 = (bf16[128,320]{0,1:T(8,128)(2,1)S(1)}, bf16[128,320]{0,1:T(8,128)(2,1)}, u32[]{:S(2)}) copy-start(bf16[128,320]{0,1:T(8,128)(2,1)} %param.9) | copy-start | bytes 245764
  29.3 55.3 %all-to-all-start = ((bf16[32,2,1,20480]{3,1,2,0:T(2,128)(2,1)}), bf16[32,2,1,20480]{3,1,2,0:T(2,128)(2,1)}, u32[]{:S(2)}, u32[]{:S(2)}) async-start(bf16[32,2,1,20480]{3,1,2,0:T(2,128)(2,1)} %bitcast.129), calls=%async_computation | async-start | bytes 5242880 | tf_op jit(solution)/shard_map/all_to_all | solution.py:184
  37.1 125.7 %reduce-scatter.2.cloned.1.call-start = ((), (), s32[]{:S(2)}) async-start(), calls=%async_computation.2 | async-start | bytes 1474560 | tf_op jit(solution)/shard_map/reduce_scatter | solution.py:197
  58.9 6.1 %collective-permute-start.2 = (bf16[128,320]{0,1:T(8,128)(2,1)S(1)}, bf16[128,320]{0,1:T(8,128)(2,1)S(1)}, u32[]{:S(2)}, u32[]{:S(2)}) collective-permute-start(bf16[128,320]{0,1:T(8,128)(2,1)S(1)} %collective-permute-done), channel_id=1, source_target_pairs={{0,1},{1,2},{2,3},{3,4},{4,5},{5,6},{6,7},{7,0},{8,9},{9,10},{10,1... | collective-permute-start | bytes 245768 | tf_op jit(solution)/shard_map/ppermute | solution.py:125
  59.0 6.6 %collective-permute-start.3 = (bf16[128,320]{0,1:T(8,128)(2,1)S(1)}, bf16[128,320]{0,1:T(8,128)(2,1)S(1)}, u32[]{:S(2)}, u32[]{:S(2)}) collective-permute-start(bf16[128,320]{0,1:T(8,128)(2,1)S(1)} %collective-permute-done.1), channel_id=1, source_target_pairs={{0,7},{1,0},{2,1},{3,2},{4,3},{5,4},{6,5},{7,6},{8,15},{9,8},{10,9... | collective-permute-start | bytes 245768 | tf_op jit(solution)/shard_map/ppermute | solution.py:130
  65.0 5.7 %copy-start.5 = (bf16[128,320]{0,1:T(8,128)(2,1)}, bf16[128,320]{0,1:T(8,128)(2,1)S(1)}, u32[]{:S(2)}) copy-start(bf16[128,320]{0,1:T(8,128)(2,1)S(1)} %collective-permute-done.2) | copy-start | bytes 245764
  65.0 5.7 %collective-permute-start.4 = (bf16[128,320]{0,1:T(8,128)(2,1)S(1)}, bf16[128,320]{0,1:T(8,128)(2,1)S(1)}, u32[]{:S(2)}, u32[]{:S(2)}) collective-permute-start(bf16[128,320]{0,1:T(8,128)(2,1)S(1)} %collective-permute-done.2), channel_id=1, source_target_pairs={{0,1},{1,2},{2,3},{3,4},{4,5},{5,6},{6,7},{7,0},{8,9},{9,10},{10,1... | collective-permute-start | bytes 245768 | tf_op jit(solution)/shard_map/ppermute | solution.py:125
  65.6 11.7 %collective-permute-start.5 = (bf16[128,320]{0,1:T(8,128)(2,1)S(1)}, bf16[128,320]{0,1:T(8,128)(2,1)}, u32[]{:S(2)}, u32[]{:S(2)}) collective-permute-start(bf16[128,320]{0,1:T(8,128)(2,1)S(1)} %collective-permute-done.3), channel_id=1, source_target_pairs={{0,7},{1,0},{2,1},{3,2},{4,3},{5,4},{6,5},{7,6},{8,15},{9,8},{10,9... | collective-permute-start | bytes 245768 | tf_op jit(solution)/shard_map/ppermute | solution.py:130
  70.6 8.8 %collective-permute-start.6 = (bf16[128,320]{0,1:T(8,128)(2,1)S(1)}, bf16[128,320]{0,1:T(8,128)(2,1)}, u32[]{:S(2)}, u32[]{:S(2)}) collective-permute-start(bf16[128,320]{0,1:T(8,128)(2,1)S(1)} %collective-permute-done.4), channel_id=1, source_target_pairs={{0,1},{1,2},{2,3},{3,4},{4,5},{5,6},{6,7},{7,0},{8,9},{9,10},{10,1... | collective-permute-start | bytes 245768 | tf_op jit(solution)/shard_map/ppermute | solution.py:125
  71.3 10.1 %copy-start.10 = (f32[2560]{0:T(1024)S(1)}, f32[2560]{0:T(1024)}, u32[]{:S(2)}) copy-start(f32[2560]{0:T(1024)} %param.10) | copy-start | bytes 30724
  77.3 5.8 %copy-start.9 = (f32[40]{0:T(128)S(1)}, f32[40]{0:T(128)}, u32[]{:S(2)}) copy-start(f32[40]{0:T(128)} %negate_power_fusion) | copy-start | bytes 484
  99.2 6.0 %copy-start.1 = (pred[2,32,64,128]{3,2,1,0:T(8,128)(4,1)S(1)}, pred[2,32,64,128]{3,2,1,0:T(8,128)(4,1)}, u32[]{:S(2)}) copy-start(pred[2,32,64,128]{3,2,1,0:T(8,128)(4,1)} %fusion.9) | copy-start | bytes 1572868
  109.2 5.9 %copy-start.2 = (bf16[2,16,1,128,2,80]{3,5,1,0,4,2:T(8,128)(2,1)S(1)}, bf16[2,16,1,128,2,80]{3,5,1,0,4,2:T(8,128)(2,1)}, u32[]{:S(2)}) copy-start(bf16[2,16,1,128,2,80]{3,5,1,0,4,2:T(8,128)(2,1)} %copy.115) | copy-start | bytes 3932164
  109.2 5.9 %copy-start.3 = (bf16[2,16,1,128,2,80]{3,5,1,0,4,2:T(8,128)(2,1)S(1)}, bf16[2,16,1,128,2,80]{3,5,1,0,4,2:T(8,128)(2,1)}, u32[]{:S(2)}) copy-start(bf16[2,16,1,128,2,80]{3,5,1,0,4,2:T(8,128)(2,1)} %copy.116) | copy-start | bytes 3932164
  115.2 5.1 %copy-start.6 = (bf16[128,1,1,80]{3,0,2,1:T(8,128)(2,1)S(1)}, bf16[128,1,1,80]{3,0,2,1:T(8,128)(2,1)}, u32[]{:S(2)}) copy-start(bf16[128,1,1,80]{3,0,2,1:T(8,128)(2,1)} %copy.129) | copy-start | bytes 61444
Sparse Core Ops, SparseCore 0:
  124.5 38.2 reduce-scatter.1
